TPU v7x, 512 devices: a whole 4x8x8 slice. The times are simulated.
512 devices in a mesh: bulk: 128 (over y, z, core), rep: 4 (over x).
Axes of the slice: x: 4, y: 8, z: 8, core: 2. Of those that a mesh axis runs over, the one named last changes fastest.
Arguments:
- orbitals: float32 [16384, 2048], P('rep', 'bulk'), may hold values from -6 to 6
- triangles: float32 [1024, 1024], P('rep', 'bulk'), may hold values from -0.09375 to 0.09375
- coupling: float32 [1024, 1024], P('rep', 'bulk'), may hold values from -0.09375 to 0.09375
- diagonals: float32 [2, 1024], P(None, 'bulk'), may hold values from 1 to 2
Outputs:
- solved: float32 [16384, 2048], P(('rep', 'bulk'))
All inputs are finite; a program needn't handle non-finite values.
Results may differ from a plain program's by a relative error of at most 0.000084.
Values sent between devices are 32-bit elements; how exact they have to be, the bound alone decides.
A program may use at most 64 MiB of HBM per device.

v0:
```python
import jax
import jax.numpy as jnp
from jax import lax
from jax.sharding import PartitionSpec as P


def unpack(triangles, diagonals):
    first_block = jnp.tril(triangles, -1) + jnp.diag(diagonals[0])
    second_block = jnp.tril(triangles.T, -1) + jnp.diag(diagonals[1])
    return (first_block, second_block)


def per_device(orbitals, triangles, coupling, diagonals):
    tri_rows, couple_rows = (
        lax.all_gather(triangles, "rep", axis=0, tiled=True),
        lax.all_gather(coupling, "rep", axis=0, tiled=True),
    )
    tri_whole, couple_whole, diag_whole = (
        lax.all_gather(tri_rows, "bulk", axis=1, tiled=True),
        lax.all_gather(couple_rows, "bulk", axis=1, tiled=True),
        lax.all_gather(diagonals, "bulk", axis=1, tiled=True),
    )
    first_block, second_block = unpack(tri_whole, diag_whole)
    panel = first_block.shape[0]
    groups = lax.axis_size("bulk")
    local_rows = orbitals.shape[0] // groups
    blocks = orbitals.reshape(groups, local_rows, orbitals.shape[1])
    received = lax.all_to_all(blocks, "bulk", split_axis=0, concat_axis=2, tiled=True)
    count = received.shape[1]
    full_width = received.shape[2]
    rows_now = received.reshape(count, full_width)
    left_part = rows_now[:, :panel]
    right_part = rows_now[:, panel:]
    solved_one = jax.scipy.linalg.solve_triangular(first_block, left_part.T, lower=True).T
    update = jnp.dot(
        solved_one,
        couple_whole.T,
        precision=lax.Precision.HIGHEST,
        preferred_element_type=jnp.float32,
    )
    solved_two = jax.scipy.linalg.solve_triangular(
        second_block, (right_part - update).T, lower=True
    ).T
    joined = jnp.concatenate([solved_one, solved_two], axis=1)
    result = joined.reshape(1, count, full_width)
    return result.reshape(local_rows, result.shape[2])


def solution(mesh):
    return jax.shard_map(
        per_device,
        mesh=mesh,
        in_specs=(P("rep", "bulk"), P("rep", "bulk"), P("rep", "bulk"), P(None, "bulk")),
        out_specs=P(("rep", "bulk"), None),
        check_vma=False,
    )
```

profile of v0, /device:TPU:1, one launch (start us, length us, event | category | flops | bytes accessed | tf_op | source)
XLA Modules:
  0.0 365.9 jit_solution(3939326885254710032)
XLA Ops:
  6.5 11.9 %all_gather.15 = f32[1024,8]{0,1:T(8,128)} all-gather(f32[256,8]{0,1:T(8,128)} %param.7), channel_id=1, replica_groups=mesh['bulk'=128,'rep'=4] {'rep'}, dimensions={0}, use_global_device_ids=true | all-gather | bytes 40960 | tf_op jit(solution)/shard_map/all_gather | solution.py:15
  21.6 20.3 %all-to-all-start = ((f32[128,1,512]{2,1,0:T(1,128)}), f32[128,1,512]{2,1,0:T(1,128)S(1)}, u32[]{:S(2)}, u32[]{:S(2)}) async-start(f32[128,1,512]{2,1,0:T(1,128)} %reshape.53), calls=%async_computation | async-start | bytes 524288 | tf_op jit(solution)/shard_map/all_to_all | solution.py:28
  41.9 10.3 %all_gather.18 = f32[1024,8]{0,1:T(8,128)} all-gather(f32[256,8]{0,1:T(8,128)S(1)} %copy-done.1), channel_id=1, replica_groups=mesh['bulk'=128,'rep'=4] {'rep'}, dimensions={0}, use_global_device_ids=true | all-gather | bytes 40960 | tf_op jit(solution)/shard_map/all_gather | solution.py:16
  53.1 53.9 %all-gather = f32[128,8,2]{1,2,0:T(2,128)S(1)} all-gather(f32[1,8,2]{1,2,0:T(2,128)S(1)} %bitcast.165), channel_id=1, replica_groups=mesh['bulk'=128,'rep'=4] {'bulk'}, dimensions={0}, use_global_device_ids=true | all-gather | bytes 8256 | tf_op jit(solution)/shard_map/all_gather | solution.py:21
  107.1 2.0 copy.25
  109.3 2.0 copy.26
  112.6 2.2 reduce
  118.7 5.0 %add_select_fusion = f32[1024,1024]{0,1:T(8,128)} fusion(f32[1024,1024]{0,1:T(8,128)} %all-gather.4.cloned.1.call-done, f32[1024]{0:T(1024)S(1)} %bitcast.163, s32[1024]{0:T(1024)S(1)} %iota_add_fusion), kind=kLoop, calls=%fused_computation.9 | loop fusion | flops 7340032 | bytes 8396800 | tf_op jit(solution)/shard_map/jit(_solve_triangular)/triangular_solve | solution.py:34
  123.7 23.5 %while.4 = (s32[]{:T(128)}, f32[1024,1024]{0,1:T(8,128)}, s32[8,2]{0,1:T(2,128)S(1)}, f32[8,128,128]{2,1,0:T(8,128)S(1)}, s32[]{:T(128)}) while((s32[]{:T(128)}, f32[1024,1024]{0,1:T(8,128)}, s32[8,2]{0,1:T(2,128)S(1)}, f32[8,128,128]{2,1,0:T(8,128)S(1)}, s32[]{:T(128)}) %tuple.84), condition=%wide.while_cond, body=%wide.while_body.sunk | while | flops 2 | bytes 393329 | solution.py:34
  124.3 2.2 dynamic-slice.13
  127.2 2.2 dynamic-slice.13
  130.2 2.2 dynamic-slice.13
  133.1 2.2 dynamic-slice.13
  136.0 2.2 dynamic-slice.13
  139.0 2.2 dynamic-slice.13
  141.9 2.2 dynamic-slice.13
  144.9 2.1 dynamic-slice.13
  147.1 78.6 %custom-call.4 = f32[8,128,128]{1,2,0:T(8,128)S(1)} custom-call(f32[8,128,128]{2,1,0:T(8,128)S(1)} %get-tuple-element.20), custom_call_target="InvertDiagBlocksLowerTriangular" | custom-call | tf_op jit(solution)/shard_map/jit(_solve_triangular)/triangular_solve | solution.py:34
  225.7 5.1 %fusion.1 = f32[1024,1024]{1,0:T(8,128)} fusion(pred[1024,1024]{1,0:T(8,128)(4,1)S(1)} %copy.25, f32[1024,1024]{0,1:T(8,128)} %all-gather.4.cloned.1.call-done, pred[1024,1024]{1,0:T(8,128)(4,1)S(1)} %copy.26, f32[1024]{0:T(1024)S(1)} %bitcast.164), kind=kLoop, calls=%fused_computation.6 | loop fusion | flops 5242880 | bytes 10489856 | tf_op jit(solution)/shard_map/jit(_solve_triangular)/triangular_solve | solution.py:41
  230.8 23.2 %while.5 = (s32[]{:T(128)}, f32[1024,1024]{1,0:T(8,128)}, s32[8,2]{0,1:T(2,128)S(1)}, f32[8,128,128]{2,1,0:T(8,128)S(1)}, s32[]{:T(128)}) while((s32[]{:T(128)}, f32[1024,1024]{1,0:T(8,128)}, s32[8,2]{0,1:T(2,128)S(1)}, f32[8,128,128]{2,1,0:T(8,128)S(1)}, s32[]{:T(128)}) %tuple.94), condition=%wide.while_cond.clone, body=%wide.while_body.clone.sunk | while | flops 2 | bytes 131189 | solution.py:41
  231.5 2.3 bitcast_dynamic-update-slice_fusion.5
  234.4 2.3 bitcast_dynamic-update-slice_fusion.5
  237.3 2.3 bitcast_dynamic-update-slice_fusion.5
  240.2 2.3 bitcast_dynamic-update-slice_fusion.5
  243.1 2.3 bitcast_dynamic-update-slice_fusion.5
  246.0 2.3 bitcast_dynamic-update-slice_fusion.5
  248.9 2.3 bitcast_dynamic-update-slice_fusion.5
  251.8 2.2 bitcast_dynamic-update-slice_fusion.5
  254.1 78.8 %custom-call.5 = f32[8,128,128]{1,2,0:T(8,128)S(1)} custom-call(f32[8,128,128]{2,1,0:T(8,128)S(1)} %get-tuple-element.21), custom_call_target="InvertDiagBlocksLowerTriangular" | custom-call | tf_op jit(solution)/shard_map/jit(_solve_triangular)/triangular_solve | solution.py:41
  342.9 4.7 %fusion.2 = f32[1024,32]{0,1:T(8,128)S(1)} fusion(f32[32,1024]{1,0:T(8,128)S(1)} %copy.30, f32[1024,32]{0,1:T(8,128)S(1)} %convolution_dynamic-update-slice_fusion.1, f32[1024,1024]{0,1:T(8,128)} %all-gather.6.cloned.1.call-done), kind=kOutput, calls=%fused_computation.13 | convolution fusion | flops 402685952 | bytes 4587520 | tf_op jit(solution)/shard_map/dot_general | solution.py:35
  354.9 1.5 convolution_subtract_fusion.10
  356.5 1.6 convolution_subtract_fusion.9
  (108 shorter events, 38.2 us)
Async XLA Ops:
  6.5 35.3 %copy-start.1 = (f32[256,8]{0,1:T(8,128)S(1)}, f32[256,8]{0,1:T(8,128)}, u32[]{:S(2)}) copy-start(f32[256,8]{0,1:T(8,128)} %param.8) | copy-start | bytes 24580
  6.5 46.5 %copy-start.2 = (f32[2,8]{1,0:T(2,128)S(1)}, f32[2,8]{1,0:T(2,128)}, u32[]{:S(2)}) copy-start(f32[2,8]{1,0:T(2,128)} %param.9) | copy-start | bytes 196
  6.5 112.1 %all-gather.4.cloned.1.call-start = ((), (), s32[]{:S(2)}) async-start(), calls=%async_computation.1 | async-start | bytes 4227072 | tf_op jit(solution)/shard_map/all_gather | solution.py:19
  21.6 89.8 %all-to-all-start = ((f32[128,1,512]{2,1,0:T(1,128)}), f32[128,1,512]{2,1,0:T(1,128)S(1)}, u32[]{:S(2)}, u32[]{:S(2)}) async-start(f32[128,1,512]{2,1,0:T(1,128)} %reshape.53), calls=%async_computation | async-start | bytes 524288 | tf_op jit(solution)/shard_map/all_to_all | solution.py:28
  41.8 301.1 %all-gather.6.cloned.1.call-start = ((), (), s32[]{:S(2)}) async-start(), calls=%async_computation.2 | async-start | bytes 4227072 | tf_op jit(solution)/shard_map/all_gather | solution.py:20
  111.4 0.7 copy-start
Sparse Core Ops, SparseCore 0:
  18.6 93.3 all-gather.3
  115.1 82.0 all-gather.5
where the time goes:
time: 368 us; the launch traced here: 366 us
  other arithmetic  171 us (46%)
  blocking collectives  76.1 us (21%)
  local copies, waits for them, and re-layouts  58.5 us (16%)
  matrix products  25.1 us (7%)
  starting transfers between devices  20.3 us (6%)
  between operations  13.8 us (4%)
    another operation x2, other arithmetic, per_device(): jax.scipy.linalg.solve_triangular(second_block, (right_part - update).T,...  83.9 us
    another operation x3, other arithmetic, per_device(): jax.scipy.linalg.solve_triangular(first_block, left_part.T, lower=True)  83.5 us
    all_gather x1, blocking collectives, per_device(): lax.all_gather(diagonals, 'bulk', axis=1, tiled=True)  53.9 us
    another operation x43, local copies, waits for them, and re-layouts, per_device(): jax.scipy.linalg.solve_triangular(first_block, left_part.T, lower=True)  23.3 us
    another operation x24, local copies, waits for them, and re-layouts, per_device(): jax.scipy.linalg.solve_triangular(second_block, (right_part - update).T,...  23.1 us
    all_to_all x1, starting transfers between devices, per_device(): lax.all_to_all(blocks, 'bulk', split_axis=0, concat_axis=2, tiled=True)  20.3 us
    all_gather x1, blocking collectives, per_device(): lax.all_gather(triangles, 'rep', axis=0, tiled=True)  11.9 us
    another operation x15, matrix products, per_device(): jax.scipy.linalg.solve_triangular(second_block, (right_part - update).T,...  10.6 us
  transfers between devices with their start and end apart: 3, of which 0 were waited for; matrix products, arithmetic and copies ran while one was open for 65% of the time, Pallas kernels for 0%

commit v1 on v0

--- a/solution.py
+++ b/solution.py
@@ -25,7 +25,10 @@
     groups = lax.axis_size("bulk")
     local_rows = orbitals.shape[0] // groups
     blocks = orbitals.reshape(groups, local_rows, orbitals.shape[1])
-    received = lax.all_to_all(blocks, "bulk", split_axis=0, concat_axis=2, tiled=True)
+    received = jnp.concatenate(
+        lax.all_to_all(jnp.stack(jnp.split(blocks, lax.axis_size("bulk"), axis=0)), "bulk", 0, 0),
+        axis=2,
+    )
     count = received.shape[1]
     full_width = received.shape[2]
     rows_now = received.reshape(count, full_width)

time: 368 us -> 469 us (1.27)
  local copies, waits for them, and re-layouts: 58.5 us -> 155 us
    unnamed x11 -> x136, local copies, waits for them, and re-layouts: 4.67 us -> 100 us
  transfers between devices with their start and end apart: 3 -> 3, of which waited for: 0 -> 0; matrix products, arithmetic and copies ran while one was open for 65% -> 72% of each run, Pallas kernels for 0% -> 0%
where the time goes in v1:
time: 469 us; the launch traced here: 462 us
  other arithmetic  172 us (37%)
  local copies, waits for them, and re-layouts  155 us (33%)
  blocking collectives  76.4 us (16%)
  matrix products  25.1 us (5%)
  starting transfers between devices  20.1 us (4%)
  between operations  13.9 us (3%)
    unnamed x136, local copies, waits for them, and re-layouts  100 us
    another operation x2, other arithmetic, per_device(): jax.scipy.linalg.solve_triangular(second_block, (right_part - update).T,...  83.9 us
    another operation x3, other arithmetic, per_device(): jax.scipy.linalg.solve_triangular(first_block, left_part.T, lower=True)  83.6 us
    all_gather x1, blocking collectives, per_device(): lax.all_gather(diagonals, 'bulk', axis=1, tiled=True)  53.6 us
    another operation x43, local copies, waits for them, and re-layouts, per_device(): jax.scipy.linalg.solve_triangular(first_block, left_part.T, lower=True)  24.7 us
    another operation x24, local copies, waits for them, and re-layouts, per_device(): jax.scipy.linalg.solve_triangular(second_block, (right_part - update).T,...  23.4 us
    all_to_all x1, starting transfers between devices, per_device(): lax.all_to_all(jnp.stack(jnp.split(blocks, lax.axis_size('bulk'), axis=0)...  20 us
    all_gather x1, blocking collectives, per_device(): lax.all_gather(triangles, 'rep', axis=0, tiled=True)  12.1 us
  transfers between devices with their start and end apart: 3, of which 0 were waited for; matrix products, arithmetic and copies ran while one was open for 72% of the time, Pallas kernels for 0%

profile of v1, /device:TPU:1, one launch (start us, length us, event | category | flops | bytes accessed | tf_op | source)
XLA Modules:
  0.0 462.3 jit_solution(5996929328359170207)
XLA Ops:
  6.5 12.1 %all_gather.15 = f32[1024,8]{0,1:T(8,128)} all-gather(f32[256,8]{0,1:T(8,128)} %param.7), channel_id=1, replica_groups=mesh['bulk'=128,'rep'=4] {'rep'}, dimensions={0}, use_global_device_ids=true | all-gather | bytes 40960 | tf_op jit(solution)/shard_map/all_gather | solution.py:15
  116.1 20.0 %all-to-all-start = ((f32[128,1,512]{2,1,0:T(1,128)}), f32[128,1,512]{2,1,0:T(1,128)S(1)}, u32[]{:S(2)}, u32[]{:S(2)}) async-start(f32[128,1,512]{2,1,0:T(1,128)} %reshape.305), calls=%async_computation | async-start | bytes 524288 | tf_op jit(solution)/shard_map/all_to_all | solution.py:29
  136.2 10.7 %all_gather.18 = f32[1024,8]{0,1:T(8,128)} all-gather(f32[256,8]{0,1:T(8,128)} %param.8), channel_id=1, replica_groups=mesh['bulk'=128,'rep'=4] {'rep'}, dimensions={0}, use_global_device_ids=true | all-gather | bytes 40960 | tf_op jit(solution)/shard_map/all_gather | solution.py:16
  147.8 53.6 %all-gather = f32[128,8,2]{1,2,0:T(2,128)S(1)} all-gather(f32[1,8,2]{1,2,0:T(2,128)S(1)} %bitcast.415), channel_id=1, replica_groups=mesh['bulk'=128,'rep'=4] {'bulk'}, dimensions={0}, use_global_device_ids=true | all-gather | bytes 8256 | tf_op jit(solution)/shard_map/all_gather | solution.py:21
  201.6 2.0 copy.572
  203.9 2.0 copy.573
  207.1 2.2 reduce
  213.3 5.0 %add_select_fusion = f32[1024,1024]{0,1:T(8,128)} fusion(f32[1024,1024]{0,1:T(8,128)} %all-gather.4.cloned.1.call-done, f32[1024]{0:T(1024)S(1)} %bitcast.413, s32[1024]{0:T(1024)S(1)} %iota_add_fusion), kind=kLoop, calls=%fused_computation.9 | loop fusion | flops 7340032 | bytes 8396800 | tf_op jit(solution)/shard_map/jit(_solve_triangular)/triangular_solve | solution.py:37
  218.3 24.9 %while.4 = (s32[]{:T(128)}, f32[1024,1024]{0,1:T(8,128)}, s32[8,2]{0,1:T(2,128)S(1)}, f32[8,128,128]{2,1,0:T(8,128)S(1)}, s32[]{:T(128)}) while((s32[]{:T(128)}, f32[1024,1024]{0,1:T(8,128)}, s32[8,2]{0,1:T(2,128)S(1)}, f32[8,128,128]{2,1,0:T(8,128)S(1)}, s32[]{:T(128)}) %tuple.88), condition=%wide.while_cond, body=%wide.while_body.sunk | while | flops 2 | bytes 393329 | solution.py:37
  219.0 2.3 dynamic-slice.13
  222.1 2.3 dynamic-slice.13
  225.2 2.3 dynamic-slice.13
  228.3 2.3 dynamic-slice.13
  231.4 2.3 dynamic-slice.13
  234.6 2.3 dynamic-slice.13
  237.7 2.3 dynamic-slice.13
  240.8 2.3 dynamic-slice.13
  243.2 78.6 %custom-call.4 = f32[8,128,128]{1,2,0:T(8,128)S(1)} custom-call(f32[8,128,128]{2,1,0:T(8,128)S(1)} %get-tuple-element.20), custom_call_target="InvertDiagBlocksLowerTriangular" | custom-call | tf_op jit(solution)/shard_map/jit(_solve_triangular)/triangular_solve | solution.py:37
  321.8 5.1 %fusion.1 = f32[1024,1024]{1,0:T(8,128)} fusion(pred[1024,1024]{1,0:T(8,128)(4,1)S(1)} %copy.572, f32[1024,1024]{0,1:T(8,128)} %all-gather.4.cloned.1.call-done, pred[1024,1024]{1,0:T(8,128)(4,1)S(1)} %copy.573, f32[1024]{0:T(1024)S(1)} %bitcast.414), kind=kLoop, calls=%fused_computation.6 | loop fusion | flops 5242880 | bytes 10489856 | tf_op jit(solution)/shard_map/jit(_solve_triangular)/triangular_solve | solution.py:44
  326.9 23.6 %while.5 = (s32[]{:T(128)}, f32[1024,1024]{1,0:T(8,128)}, s32[8,2]{0,1:T(2,128)S(1)}, f32[8,128,128]{2,1,0:T(8,128)S(1)}, s32[]{:T(128)}) while((s32[]{:T(128)}, f32[1024,1024]{1,0:T(8,128)}, s32[8,2]{0,1:T(2,128)S(1)}, f32[8,128,128]{2,1,0:T(8,128)S(1)}, s32[]{:T(128)}) %tuple.98), condition=%wide.while_cond.clone, body=%wide.while_body.clone.sunk | while | flops 2 | bytes 131189 | solution.py:44
  327.5 2.3 bitcast_dynamic-update-slice_fusion.5
  330.5 2.3 bitcast_dynamic-update-slice_fusion.5
  333.5 2.3 bitcast_dynamic-update-slice_fusion.5
  336.4 2.3 bitcast_dynamic-update-slice_fusion.5
  339.4 2.3 bitcast_dynamic-update-slice_fusion.5
  342.3 2.3 bitcast_dynamic-update-slice_fusion.5
  345.3 2.3 bitcast_dynamic-update-slice_fusion.5
  348.2 2.2 bitcast_dynamic-update-slice_fusion.5
  350.5 78.8 %custom-call.5 = f32[8,128,128]{1,2,0:T(8,128)S(1)} custom-call(f32[8,128,128]{2,1,0:T(8,128)S(1)} %get-tuple-element.21), custom_call_target="InvertDiagBlocksLowerTriangular" | custom-call | tf_op jit(solution)/shard_map/jit(_solve_triangular)/triangular_solve | solution.py:44
  439.3 4.7 %fusion.2 = f32[1024,32]{0,1:T(8,128)S(1)} fusion(f32[32,1024]{1,0:T(8,128)S(1)} %copy.577, f32[1024,32]{0,1:T(8,128)S(1)} %convolution_dynamic-update-slice_fusion.1, f32[1024,1024]{0,1:T(8,128)} %all-gather.6.cloned.1.call-done), kind=kOutput, calls=%fused_computation.13 | convolution fusion | flops 402685952 | bytes 4587520 | tf_op jit(solution)/shard_map/dot_general | solution.py:38
  451.3 1.5 convolution_subtract_fusion.10
  452.9 1.6 convolution_subtract_fusion.9
  (232 shorter events, 133.5 us)
Async XLA Ops:
  6.5 141.2 %copy-start.1 = (f32[2,8]{1,0:T(2,128)S(1)}, f32[2,8]{1,0:T(2,128)}, u32[]{:S(2)}) copy-start(f32[2,8]{1,0:T(2,128)} %param.9) | copy-start | bytes 196
  6.5 206.7 %all-gather.4.cloned.1.call-start = ((), (), s32[]{:S(2)}) async-start(), calls=%async_computation.1 | async-start | bytes 4227072 | tf_op jit(solution)/shard_map/all_gather | solution.py:19
  116.1 89.7 %all-to-all-start = ((f32[128,1,512]{2,1,0:T(1,128)}), f32[128,1,512]{2,1,0:T(1,128)S(1)}, u32[]{:S(2)}, u32[]{:S(2)}) async-start(f32[128,1,512]{2,1,0:T(1,128)} %reshape.305), calls=%async_computation | async-start | bytes 524288 | tf_op jit(solution)/shard_map/all_to_all | solution.py:29
  136.2 303.1 %all-gather.6.cloned.1.call-start = ((), (), s32[]{:S(2)}) async-start(), calls=%async_computation.2 | async-start | bytes 4227072 | tf_op jit(solution)/shard_map/all_gather | solution.py:20
  205.9 0.7 copy-start
Sparse Core Ops, SparseCore 0:
  18.8 91.2 all-gather.3
  147.1 86.9 all-gather.5
